TPU v7x, 256 devices: a whole 4x4x8 slice. The times are simulated.
256 devices in a mesh: dp: 32 (over z, y), fsdp: 8 (over x, core).
Axes of the slice: x: 4, y: 4, z: 8, core: 2. Of those that a mesh axis runs over, the one named last changes fastest.
Arguments:
- frames: bfloat16 [8, 768, 32, 1536], P('fsdp', 'dp'), may hold values from -6 to 6
- ln_gain: float32 [1536], replicated, may hold values from 0.5 to 1.5
- w_in: bfloat16 [1536, 3072], P(('dp', 'fsdp')), may hold values from -0.15625 to 0.15625
- depth_kernel: float32 [31, 1536], replicated, may hold values from -1 to 1
- bn_scale: float32 [1536], replicated, may hold values from 0.5 to 1.5
- bn_shift: float32 [1536], replicated, may hold values from -3 to 3
- w_out: bfloat16 [1536, 1536], P(('dp', 'fsdp')), may hold values from -0.15625 to 0.15625
- lengths: int32 [8, 32, 24], P('fsdp'), may hold values from 0 to 32, as said below
- destinations: int32 [8, 32, 24], P('fsdp'), may hold values from 0 to 31, as said below
- offsets: int32 [8, 32, 24], P('fsdp'), may hold values from 0 to 224, as said below
Outputs:
- encoded: bfloat16 [8, 256, 32, 1536], P('fsdp', 'dp')
Inputs may be any that keep to these rules, and one draw needn't show every extreme that they name: lengths: live slots come first in a loader and hold half of 32 to 32 frames; 0 marks an empty slot. In each group the busiest loader has all 24 slots live, the group has 256 live utterances, and one of them has 32 frames. destinations: within a group a loader sends at most one live utterance to a device, and every device receives exactly 8 live utterances. Empty slots hold 0. offsets: multiples of 32; the 8 live utterances received by one device have distinct offsets. Empty slots hold 0.
All inputs are finite; a program needn't handle non-finite values.
Results may differ from a plain program's by a relative error of at most 0.003.
Values may be sent and summed in bfloat16 or wider, within the bound.
A program may use at most 128 MiB of HBM per device.

v0:
```python
import jax
import jax.numpy as jnp
from jax import lax
from jax.sharding import PartitionSpec as P


def conv_module(blocks, utt_lengths, ln_gain, depth_kernel, bn_scale, bn_shift, full_in, full_out):
    block_count, frames_len, feature_width = blocks.shape
    wide_rows = blocks.reshape(block_count * frames_len, feature_width).astype(jnp.float32)
    row_mean = jnp.mean(wide_rows, axis=1, keepdims=True)
    centred = wide_rows - row_mean
    row_var = jnp.mean(centred * centred, axis=1, keepdims=True)
    normed = (centred * lax.rsqrt(row_var + 1e-05) * ln_gain).astype(jnp.bfloat16)
    glu_in = jnp.dot(normed, full_in, preferred_element_type=jnp.float32)
    gated_units = glu_in[:, :feature_width] * jax.nn.sigmoid(glu_in[:, feature_width:])
    gated_units = gated_units.reshape(block_count, frames_len, feature_width)
    valid_mask = jnp.arange(frames_len, dtype=jnp.int32)[None, :] < utt_lengths[:, None]
    gated_units = jnp.where(valid_mask[:, :, None], gated_units, jnp.zeros((), gated_units.dtype))
    side_reach = (depth_kernel.shape[0] - 1) // 2
    padded = jnp.pad(gated_units, ((0, 0), (side_reach, side_reach), (0, 0)))
    convolved = padded[:, 0:frames_len, :] * depth_kernel[0]
    for kernel_tap in range(1, depth_kernel.shape[0]):
        convolved = (
            convolved
            + padded[:, kernel_tap : kernel_tap + frames_len, :] * depth_kernel[kernel_tap]
        )
    shifted = convolved * bn_scale + bn_shift
    activated = (shifted * jax.nn.sigmoid(shifted)).astype(jnp.bfloat16)
    activated = activated.reshape(block_count * frames_len, feature_width)
    mixed_out = wide_rows + jnp.dot(activated, full_out, preferred_element_type=jnp.float32)
    mixed_out = mixed_out.reshape(block_count, frames_len, feature_width)
    mixed_out = jnp.where(valid_mask[:, :, None], mixed_out, jnp.zeros((), mixed_out.dtype))
    return mixed_out.astype(jnp.bfloat16)


def shards(
    frames, ln_gain, w_in, depth_kernel, bn_scale, bn_shift, w_out, lengths, destinations, offsets
):
    dp_count = lax.axis_size("dp")
    dp_index = lax.axis_index("dp")
    tab_len = lengths[0]
    tab_dest = destinations[0]
    tab_off = offsets[0]
    slot_count = tab_len.shape[1]
    recv_count = slot_count // 3
    frame_slots = frames.shape[2]
    own_len = lax.dynamic_index_in_dim(tab_len, dp_index, 0, keepdims=False)
    own_dest = lax.dynamic_index_in_dim(tab_dest, dp_index, 0, keepdims=False)
    slot_ids = jnp.arange(slot_count, dtype=jnp.int32)
    peer_ids = jnp.arange(dp_count, dtype=jnp.int32)
    send_table = ((own_dest[None, :] == peer_ids[:, None]) & (own_len[None, :] > 0)).astype(
        jnp.int32
    )
    send_slot = jnp.sum(send_table * slot_ids[None, :], axis=1)
    send_live = jnp.sum(send_table, axis=1) > 0
    key_table = jnp.where(tab_len > 0, tab_dest * recv_count + tab_off // frame_slots, -1)
    targets = dp_index * recv_count + jnp.arange(recv_count, dtype=jnp.int32)
    pick_table = (key_table[None, :, :] == targets[:, None, None]).astype(jnp.int32)
    recv_source = jnp.sum(pick_table * peer_ids[None, :, None], axis=(1, 2))
    full_in, full_out = (
        lax.all_gather(w_in, ("dp", "fsdp"), axis=0, tiled=True),
        lax.all_gather(w_out, ("dp", "fsdp"), axis=0, tiled=True),
    )
    local_out = conv_module(
        frames[0], own_len, ln_gain, depth_kernel, bn_scale, bn_shift, full_in, full_out
    )
    chosen = jnp.take(local_out, send_slot, axis=0)
    arrived = lax.all_to_all(
        jnp.where(send_live[:, None, None], chosen, jnp.zeros((), local_out.dtype)),
        "dp",
        split_axis=0,
        concat_axis=0,
        tiled=True,
    )
    result = jnp.take(arrived, recv_source, axis=0)
    return result[None]


def solution(mesh):
    return jax.shard_map(
        shards,
        mesh=mesh,
        in_specs=(
            P("fsdp", "dp", None, None),
            P(),
            P(("dp", "fsdp"), None),
            P(),
            P(),
            P(),
            P(("dp", "fsdp"), None),
            P("fsdp", None, None),
            P("fsdp", None, None),
            P("fsdp", None, None),
        ),
        out_specs=P("fsdp", "dp", None, None),
        check_vma=False,
    )
```

profile of v0, /device:TPU:25, one launch (start us, length us, event | category | flops | bytes accessed | tf_op | source)
XLA Modules:
  0.0 399.6 jit_solution(12368897338125634990)
XLA Ops:
  6.5 0.0 copy-start
  6.5 0.0 copy-start.2
  6.5 0.0 copy-start.3
  6.5 0.0 copy-start.1
  6.5 0.0 copy-start.5
  6.5 0.0 all-gather.7.cloned.1.call-start
  6.6 0.7 all-gather.7.cloned.1.call-update
  7.3 0.0 all-gather.5.cloned.1.call-start
  7.3 0.7 all-gather.5.cloned.1.call-update
  8.0 2.1 convert_reduce_fusion
  10.1 0.1 div.31
  10.2 2.4 fusion.67
  12.6 0.1 rsqrt.12
  12.7 0.0 copy-done.2
  12.7 0.2 dynamic-slice_reduce_fusion
  12.9 0.0 copy-done.3
  12.9 0.2 dynamic-slice_reduce_fusion.1
  13.1 0.1 convert_reduce_fusion.1
  13.2 0.0 copy-done.1
  13.2 0.2 slice_reduce_fusion.29
  13.4 0.3 slice_reduce_fusion.30
  13.7 0.1 iota_compare_fusion
  13.8 0.0 copy-done
  13.8 0.0 copy-done.5
  13.8 2.2 fusion.70
  16.0 114.2 %all-gather.7.cloned.1.call-done = bf16[256,6,1536]{2,1,0:T(8,128)(2,1)} async-done(((bf16[1,6,1536]{2,1,0:T(8,128)(2,1)}), bf16[256,6,1536]{2,1,0:T(8,128)(2,1)}) %all-gather.7.cloned.1.call-update) | async-done | bytes 4718608 | tf_op jit(solution)/shard_map/all_gather | solution.py:62
  130.2 8.5 %reshape.188 = bf16[1536,1536]{1,0:T(8,128)(2,1)} reshape(bf16[256,6,1536]{2,1,0:T(8,128)(2,1)} %all-gather.7.cloned.1.call-done) | data formatting | bytes 9437184
  138.6 113.5 %all-gather.5.cloned.1.call-done = bf16[256,6,3072]{2,1,0:T(8,128)(2,1)} async-done(((bf16[1,6,3072]{2,1,0:T(8,128)(2,1)}), bf16[256,6,3072]{2,1,0:T(8,128)(2,1)}) %all-gather.5.cloned.1.call-update) | async-done | bytes 9437200 | tf_op jit(solution)/shard_map/all_gather | solution.py:61
  252.1 14.2 %reshape.186 = bf16[1536,3072]{1,0:T(8,128)(2,1)} reshape(bf16[256,6,3072]{2,1,0:T(8,128)(2,1)} %all-gather.5.cloned.1.call-done) | data formatting | bytes 18874368
  266.3 10.7 %fusion.79 = f32[768,3072]{1,0:T(8,128)S(1)} fusion(bf16[768,1536]{1,0:T(8,128)(2,1)} %fusion.70, bf16[1536,3072]{1,0:T(8,128)(2,1)} %reshape.186), kind=kOutput, calls=%fused_computation.177 | convolution fusion | flops 7247757312 | bytes 21233664 | tf_op jit(solution)/shard_map/dot_general | solution.py:14
  277.0 1.2 fusion.65
  278.2 0.0 slice-start
  278.3 0.0 copy-start.6
  278.3 0.0 copy-start.7
  278.3 0.0 slice-start.1
  278.3 0.4 broadcast_select_fusion
  278.7 0.4 copy-done.6
  279.1 0.0 copy-done.7
  279.1 17.8 %multiply_convert_fusion = bf16[24,32,1536]{2,1,0:T(8,128)(2,1)S(1)} fusion(f32[24,32,1536]{2,1,0:T(8,128)S(1)} %broadcast_select_fusion, f32[1536]{0:T(1024)S(1)} %copy-done.6, f32[1536]{0:T(1024)S(1)} %copy-done.7, f32[1536]{0:T(1024)S(1)} %get-tuple-element.34, f32[1536]{0:T(1024)S(1)} %get-tuple-element.35, f32[1536]{0:T(1024)S(1)} %get-tuple-element.6, ...), kind=kLoop, calls=%fused_computation.109 | loop fusion | flops 80216064 | bytes 7280640 | tf_op jit(solution)/shard_map/convert_element_type | solution.py:28
  297.0 0.0 slice-done
  297.0 0.0 slice-done.1
  297.0 4.0 %bitcast_add_fusion = bf16[768,1536]{1,0:T(8,128)(2,1)S(1)} fusion(bf16[1,24,32,1536]{3,2,1,0:T(8,128)(2,1)S(1)} %copy-done, bf16[768,1536]{1,0:T(8,128)(2,1)S(1)} %bitcast.34, bf16[1536,1536]{1,0:T(8,128)(2,1)S(1)} %bitcast.32), kind=kOutput, calls=%fused_computation.99 | convolution fusion | flops 3627417600 | bytes 11796480 | tf_op jit(solution)/shard_map/dot_general | solution.py:30
  301.1 0.5 select_convert_fusion
  301.5 2.5 gather_fusion
  304.0 4.0 %select_select_fusion = bf16[32,32,1536]{2,1,0:T(8,128)(2,1)} fusion(bf16[32,32,1536]{2,1,0:T(8,128)(2,1)} %gather_fusion, pred[32]{0:T(512)(128)(4,1)S(1)} %get-tuple-element.38, pred[32]{0:T(512)(128)(4,1)S(1)} %get-tuple-element.39), kind=kLoop, calls=%fused_computation.110 | loop fusion | flops 3145728 | bytes 6291520 | tf_op jit(solution)/shard_map/jit(_where)/select_n | solution.py:69
  308.0 0.0 copy-start.4
  308.0 7.1 %all-to-all-start = ((bf16[32,32,1536]{2,1,0:T(8,128)(2,1)}), bf16[32,32,1536]{2,1,0:T(8,128)(2,1)}, u32[]{:S(2)}, u32[]{:S(2)}) async-start(bf16[32,32,1536]{2,1,0:T(8,128)(2,1)} %select_select_fusion), calls=%async_computation | async-start | bytes 6291456 | tf_op jit(solution)/shard_map/all_to_all | solution.py:68
  315.1 0.0 copy-done.4
  315.2 0.3 select_reduce_fusion
  315.5 73.8 %all-to-all-done = bf16[32,32,1536]{2,1,0:T(8,128)(2,1)} async-done(((bf16[32,32,1536]{2,1,0:T(8,128)(2,1)}), bf16[32,32,1536]{2,1,0:T(8,128)(2,1)}, u32[]{:S(2)}, u32[]{:S(2)}) %all-to-all-start) | async-done | bytes 3145760 | tf_op jit(solution)/shard_map/all_to_all | solution.py:68
  389.3 2.5 gather_fusion.1
  391.8 1.0 bitcast_select_fusion
  (12 shorter events, 0.1 us)
Async XLA Ops:
  6.5 7.3 %copy-start = (bf16[1,24,32,1536]{3,2,1,0:T(8,128)(2,1)S(1)}, bf16[1,24,32,1536]{3,2,1,0:T(8,128)(2,1)}, u32[]{:S(2)}) copy-start(bf16[1,24,32,1536]{3,2,1,0:T(8,128)(2,1)} %param.10) | copy-start | bytes 7077892
  6.5 6.1 %copy-start.2 = (s32[1,32,24]{1,2,0:T(8,128)S(1)}, s32[1,32,24]{1,2,0:T(8,128)}, u32[]{:S(2)}) copy-start(s32[1,32,24]{1,2,0:T(8,128)} %param.17) | copy-start | bytes 9220
  6.5 6.3 %copy-start.3 = (s32[1,32,24]{1,2,0:T(8,128)S(1)}, s32[1,32,24]{1,2,0:T(8,128)}, u32[]{:S(2)}) copy-start(s32[1,32,24]{1,2,0:T(8,128)} %param.18) | copy-start | bytes 9220
  6.5 6.7 %copy-start.1 = (f32[31,1536]{1,0:T(8,128)S(1)}, f32[31,1536]{1,0:T(8,128)}, u32[]{:S(2)}) copy-start(f32[31,1536]{1,0:T(8,128)} %param.13) | copy-start | bytes 571396
  6.5 7.3 %copy-start.5 = (f32[1536]{0:T(1024)S(1)}, f32[1536]{0:T(1024)}, u32[]{:S(2)}) copy-start(f32[1536]{0:T(1024)} %param.11) | copy-start | bytes 18436
  6.5 123.6 %all-gather.7.cloned.1.call-start = ((), (), s32[]{:S(2)}) async-start(), calls=%async_computation.2 | async-start | bytes 6316032 | tf_op jit(solution)/shard_map/all_gather | solution.py:62
  7.3 244.8 %all-gather.5.cloned.1.call-start = ((), (), s32[]{:S(2)}) async-start(), calls=%async_computation.1 | async-start | bytes 12632064 | tf_op jit(solution)/shard_map/all_gather | solution.py:61
  278.2 18.7 %slice-start = ((s8[4718592]{0:T(1024)(128)(4,1)}), s8[4194304]{0:T(1024)(128)(4,1)S(1)}, s32[]{:S(2)}) async-start(s8[4718592]{0:T(1024)(128)(4,1)} %bitcast.31), calls=%async_computation.3 | async-start | bytes 8388608
  278.3 0.8 copy-start.6
  278.3 0.9 copy-start.7
  278.3 18.7 %slice-start.1 = ((s8[4718592]{0:T(1024)(128)(4,1)}), s8[524288]{0:T(1024)(128)(4,1)S(1)}, s32[]{:S(2)}) async-start(s8[4718592]{0:T(1024)(128)(4,1)} %bitcast.31), calls=%async_computation.4 | async-start | bytes 1048576
  308.0 7.1 %copy-start.4 = (s32[1,32,24]{1,2,0:T(8,128)S(1)}, s32[1,32,24]{1,2,0:T(8,128)}, u32[]{:S(2)}) copy-start(s32[1,32,24]{1,2,0:T(8,128)} %param.19) | copy-start | bytes 9220
  308.0 81.3 %all-to-all-start = ((bf16[32,32,1536]{2,1,0:T(8,128)(2,1)}), bf16[32,32,1536]{2,1,0:T(8,128)(2,1)}, u32[]{:S(2)}, u32[]{:S(2)}) async-start(bf16[32,32,1536]{2,1,0:T(8,128)(2,1)} %select_select_fusion), calls=%async_computation | async-start | bytes 6291456 | tf_op jit(solution)/shard_map/all_to_all | solution.py:68
Sparse Core Ops, SparseCore 0:
  11.1 119.0 all-gather.6
  133.9 118.1 all-gather.4
where the time goes:
time: 400 us
  waiting for transfers between devices  303 us (76%)
  other arithmetic  32.1 us (8%)
  local copies, waits for them, and re-layouts  29.1 us (7%)
  matrix products  14.8 us (4%)
  between operations  13.6 us (3%)
  starting transfers between devices  7.2 us (2%)
    all_gather x1, waiting for transfers between devices, shards(): lax.all_gather(w_out, ('dp', 'fsdp'), axis=0, tiled=True)  114 us
    all_gather x1, waiting for transfers between devices, shards(): lax.all_gather(w_in, ('dp', 'fsdp'), axis=0, tiled=True)  113 us
    all_to_all x1, waiting for transfers between devices, shards(): lax.all_to_all(jnp.where(send_live[:, None, None], chosen, jnp.zeros((),...  73.8 us
    unnamed x22, local copies, waits for them, and re-layouts  23.1 us
    convert_element_type x1, other arithmetic, conv_module(): activated = (shifted * jax.nn.sigmoid(shifted)).astype(jnp.bfloat16)  17.8 us
    dot_general x1, matrix products, conv_module(): glu_in = jnp.dot(normed, full_in, preferred_element_type=jnp.float32)  10.7 us
  transfers between devices with their start and end apart: 3, of which 3 were waited for; matrix products, arithmetic and copies ran while one was open for 4% of the time, Pallas kernels for 0%

commit v1 on v0

--- a/solution.py
+++ b/solution.py
@@ -58,7 +58,10 @@
     pick_table = (key_table[None, :, :] == targets[:, None, None]).astype(jnp.int32)
     recv_source = jnp.sum(pick_table * peer_ids[None, :, None], axis=(1, 2))
     full_in, full_out = (
-        lax.all_gather(w_in, ("dp", "fsdp"), axis=0, tiled=True),
+        jnp.concatenate(
+            lax.all_to_all(jnp.stack([w_in] * lax.axis_size(("dp", "fsdp"))), ("dp", "fsdp"), 0, 0),
+            axis=0,
+        ),
         lax.all_gather(w_out, ("dp", "fsdp"), axis=0, tiled=True),
     )
     local_out = conv_module(

time: 400 us -> 464 us (1.16)
  waiting for transfers between devices: 303 us -> 345 us
  starting transfers between devices: 7.2 us -> 24.6 us
  local copies, waits for them, and re-layouts: 29.1 us -> 34.7 us
    all_to_all x0 -> x1, waiting for transfers between devices: none -> 126 us  [shards(): lax.all_to_all(jnp.stack([w_in] * lax.axis_size(('dp', 'fsdp'))), ('dp',...]
    all_gather x1 -> x0, waiting for transfers between devices: 113 us -> none  [shards(): lax.all_gather(w_in, ('dp', 'fsdp'), axis=0, tiled=True)]
    all_gather x1, waiting for transfers between devices: 114 us -> 146 us  [shards(): lax.all_gather(w_out, ('dp', 'fsdp'), axis=0, tiled=True)]
    all_to_all x0 -> x1, starting transfers between devices: none -> 15.6 us  [shards(): lax.all_to_all(jnp.stack([w_in] * lax.axis_size(('dp', 'fsdp'))), ('dp',...]
    unnamed x22 -> x21, local copies, waits for them, and re-layouts: 23.1 us -> 8.88 us
    reshape x0 -> x1, local copies, waits for them, and re-layouts: none -> 14.2 us  [shards(): jnp.concatenate(lax.all_to_all(jnp.stack([w_in] * lax.axis_size(('dp', 'f...]
    another operation x0 -> x1, local copies, waits for them, and re-layouts: none -> 6.86 us  [shards(): jnp.stack([w_in] * lax.axis_size(('dp', 'fsdp')))]
  transfers between devices with their start and end apart: 3 -> 3, of which waited for: 3 -> 3; matrix products, arithmetic and copies ran while one was open for 4% -> 3% of each run, Pallas kernels for 0% -> 0%
where the time goes in v1:
time: 464 us; the launch traced here: 462 us
  waiting for transfers between devices  345 us (74%)
  local copies, waits for them, and re-layouts  34.7 us (7%)
  other arithmetic  29.9 us (6%)
  starting transfers between devices  24.6 us (5%)
  matrix products  14.8 us (3%)
  between operations  13.7 us (3%)
    all_gather x1, waiting for transfers between devices, shards(): lax.all_gather(w_out, ('dp', 'fsdp'), axis=0, tiled=True)  146 us
    all_to_all x1, waiting for transfers between devices, shards(): lax.all_to_all(jnp.stack([w_in] * lax.axis_size(('dp', 'fsdp'))), ('dp',...  126 us
    all_to_all x1, waiting for transfers between devices, shards(): lax.all_to_all(jnp.where(send_live[:, None, None], chosen, jnp.zeros((),...  71.7 us
    convert_element_type x1, other arithmetic, conv_module(): activated = (shifted * jax.nn.sigmoid(shifted)).astype(jnp.bfloat16)  17.8 us
    all_to_all x1, starting transfers between devices, shards(): lax.all_to_all(jnp.stack([w_in] * lax.axis_size(('dp', 'fsdp'))), ('dp',...  15.6 us
    reshape x1, local copies, waits for them, and re-layouts, shards(): jnp.concatenate(lax.all_to_all(jnp.stack([w_in] * lax.axis_size(('dp', 'f...  14.2 us
    dot_general x1, matrix products, conv_module(): glu_in = jnp.dot(normed, full_in, preferred_element_type=jnp.float32)  10.7 us
  transfers between devices with their start and end apart: 3, of which 3 were waited for; matrix products, arithmetic and copies ran while one was open for 3% of the time, Pallas kernels for 0%

profile of v1, /device:TPU:25, one launch (start us, length us, event | category | flops | bytes accessed | tf_op | source)
XLA Modules:
  0.0 462.3 jit_solution(17268735930657591792)
XLA Ops:
  6.5 6.9 %stack.2 = bf16[256,6,3072]{2,1,0:T(8,128)(2,1)} broadcast(bf16[6,3072]{1,0:T(8,128)(2,1)} %param.12), dimensions={1,2} | broadcast | bytes 9474048 | tf_op jit(solution)/shard_map/stack | solution.py:62
  13.4 0.0 copy-start.2
  13.4 0.0 copy-start.3
  13.4 0.0 copy-start.1
  13.4 0.0 copy-start
  13.4 15.6 %all-to-all-start = ((bf16[256,6,3072]{2,1,0:T(8,128)(2,1)}), bf16[256,6,3072]{2,1,0:T(8,128)(2,1)}, u32[]{:S(2)}, u32[]{:S(2)}) async-start(bf16[256,6,3072]{2,1,0:T(8,128)(2,1)} %stack.2), calls=%async_computation | async-start | bytes 25165824 | tf_op jit(solution)/shard_map/all_to_all | solution.py:62
  29.0 0.0 copy-start.5
  29.1 0.2 all-gather.3.cloned.1.call-start
  29.3 0.5 all-gather.3.cloned.1.call-update
  29.8 0.0 copy-done.2
  29.8 0.2 dynamic-slice_reduce_fusion
  30.0 0.0 copy-done.3
  30.0 0.2 dynamic-slice_reduce_fusion.1
  30.2 0.1 convert_reduce_fusion.1
  30.3 0.0 copy-done.1
  30.3 0.2 slice_reduce_fusion.29
  30.5 0.3 slice_reduce_fusion.30
  30.8 0.1 iota_compare_fusion
  30.9 0.0 copy-done
  30.9 0.4 convert_reduce_fusion
  31.3 0.8 multiply_reduce_fusion
  32.1 0.0 copy-done.5
  32.1 2.2 multiply_convert_fusion.1
  34.3 146.4 %all-gather.3.cloned.1.call-done = bf16[256,6,1536]{2,1,0:T(8,128)(2,1)} async-done(((bf16[1,6,1536]{2,1,0:T(8,128)(2,1)}), bf16[256,6,1536]{2,1,0:T(8,128)(2,1)}) %all-gather.3.cloned.1.call-update) | async-done | bytes 4718608 | tf_op jit(solution)/shard_map/all_gather | solution.py:65
  180.7 8.4 %reshape.203 = bf16[1536,1536]{1,0:T(8,128)(2,1)} reshape(bf16[256,6,1536]{2,1,0:T(8,128)(2,1)} %all-gather.3.cloned.1.call-done) | data formatting | bytes 9437184
  189.1 126.0 %all-to-all-done = bf16[256,6,3072]{2,1,0:T(8,128)(2,1)} async-done(((bf16[256,6,3072]{2,1,0:T(8,128)(2,1)}), bf16[256,6,3072]{2,1,0:T(8,128)(2,1)}, u32[]{:S(2)}, u32[]{:S(2)}) %all-to-all-start) | async-done | bytes 9437216 | tf_op jit(solution)/shard_map/all_to_all | solution.py:62
  315.1 14.2 %reshape.181 = bf16[1536,3072]{1,0:T(8,128)(2,1)} reshape(bf16[256,6,3072]{2,1,0:T(8,128)(2,1)} %all-to-all-done) | data formatting | bytes 18874368 | tf_op jit(solution)/shard_map/reshape | solution.py:61
  329.3 10.7 %fusion.74 = f32[768,3072]{1,0:T(8,128)S(1)} fusion(bf16[768,1536]{1,0:T(8,128)(2,1)} %bitcast.26, bf16[1536,3072]{1,0:T(8,128)(2,1)} %reshape.181), kind=kOutput, calls=%fused_computation.172 | convolution fusion | flops 7247757312 | bytes 21233664 | tf_op jit(solution)/shard_map/dot_general | solution.py:14
  340.0 1.2 fusion.65
  341.3 0.0 slice-start
  341.3 0.0 copy-start.6
  341.3 0.0 copy-start.7
  341.3 0.0 slice-start.1
  341.3 0.4 broadcast_select_fusion
  341.7 0.4 copy-done.6
  342.1 0.0 copy-done.7
  342.2 17.8 %multiply_convert_fusion = bf16[24,32,1536]{2,1,0:T(8,128)(2,1)S(1)} fusion(f32[24,32,1536]{2,1,0:T(8,128)S(1)} %broadcast_select_fusion, f32[1536]{0:T(1024)S(1)} %copy-done.6, f32[1536]{0:T(1024)S(1)} %copy-done.7, f32[1536]{0:T(1024)S(1)} %get-tuple-element.34, f32[1536]{0:T(1024)S(1)} %get-tuple-element.35, f32[1536]{0:T(1024)S(1)} %get-tuple-element.6, ...), kind=kLoop, calls=%fused_computation.101 | loop fusion | flops 80216064 | bytes 7280640 | tf_op jit(solution)/shard_map/convert_element_type | solution.py:28
  360.0 0.0 slice-done
  360.0 0.0 slice-done.1
  360.0 4.0 bitcast_add_fusion
  364.1 0.5 select_convert_fusion
  364.6 2.4 gather_fusion
  367.0 4.0 select_select_fusion
  370.9 0.0 copy-start.4
  370.9 8.8 %all-to-all-start.1 = ((bf16[32,32,1536]{2,1,0:T(8,128)(2,1)}), bf16[32,32,1536]{2,1,0:T(8,128)(2,1)S(1)}, u32[]{:S(2)}, u32[]{:S(2)}) async-start(bf16[32,32,1536]{2,1,0:T(8,128)(2,1)} %select_select_fusion), calls=%async_computation.1 | async-start | bytes 6291456 | tf_op jit(solution)/shard_map/all_to_all | solution.py:71
  379.8 0.0 copy-done.4
  379.8 0.3 select_reduce_fusion
  380.1 71.7 %all-to-all-done.1 = bf16[32,32,1536]{2,1,0:T(8,128)(2,1)S(1)} async-done(((bf16[32,32,1536]{2,1,0:T(8,128)(2,1)}), bf16[32,32,1536]{2,1,0:T(8,128)(2,1)S(1)}, u32[]{:S(2)}, u32[]{:S(2)}) %all-to-all-start.1) | async-done | bytes 3145760 | tf_op jit(solution)/shard_map/all_to_all | solution.py:71
  451.8 1.5 gather_fusion.1
  453.3 2.2 bitcast_select_fusion
  (12 shorter events, 0.1 us)
Async XLA Ops:
  13.4 16.4 %copy-start.2 = (s32[1,32,24]{1,2,0:T(8,128)S(1)}, s32[1,32,24]{1,2,0:T(8,128)}, u32[]{:S(2)}) copy-start(s32[1,32,24]{1,2,0:T(8,128)} %param.17) | copy-start | bytes 9220
  13.4 16.6 %copy-start.3 = (s32[1,32,24]{1,2,0:T(8,128)S(1)}, s32[1,32,24]{1,2,0:T(8,128)}, u32[]{:S(2)}) copy-start(s32[1,32,24]{1,2,0:T(8,128)} %param.18) | copy-start | bytes 9220
  13.4 16.9 %copy-start.1 = (f32[31,1536]{1,0:T(8,128)S(1)}, f32[31,1536]{1,0:T(8,128)}, u32[]{:S(2)}) copy-start(f32[31,1536]{1,0:T(8,128)} %param.13) | copy-start | bytes 571396
  13.4 17.5 %copy-start = (bf16[1,24,32,1536]{3,2,1,0:T(8,128)(2,1)S(1)}, bf16[1,24,32,1536]{3,2,1,0:T(8,128)(2,1)}, u32[]{:S(2)}) copy-start(bf16[1,24,32,1536]{3,2,1,0:T(8,128)(2,1)} %param.10) | copy-start | bytes 7077892
  13.4 301.7 %all-to-all-start = ((bf16[256,6,3072]{2,1,0:T(8,128)(2,1)}), bf16[256,6,3072]{2,1,0:T(8,128)(2,1)}, u32[]{:S(2)}, u32[]{:S(2)}) async-start(bf16[256,6,3072]{2,1,0:T(8,128)(2,1)} %stack.2), calls=%async_computation | async-start | bytes 25165824 | tf_op jit(solution)/shard_map/all_to_all | solution.py:62
  29.0 3.1 copy-start.5
  29.1 151.7 %all-gather.3.cloned.1.call-start = ((), (), s32[]{:S(2)}) async-start(), calls=%async_computation.2 | async-start | bytes 6316032 | tf_op jit(solution)/shard_map/all_gather | solution.py:65
  341.3 18.7 %slice-start = ((s8[4718592]{0:T(1024)(128)(4,1)}), s8[4194304]{0:T(1024)(128)(4,1)S(1)}, s32[]{:S(2)}) async-start(s8[4718592]{0:T(1024)(128)(4,1)} %bitcast.24), calls=%async_computation.3 | async-start | bytes 8388608
  341.3 0.8 copy-start.6
  341.3 0.9 copy-start.7
  341.3 18.7 %slice-start.1 = ((s8[4718592]{0:T(1024)(128)(4,1)}), s8[524288]{0:T(1024)(128)(4,1)S(1)}, s32[]{:S(2)}) async-start(s8[4718592]{0:T(1024)(128)(4,1)} %bitcast.24), calls=%async_computation.4 | async-start | bytes 1048576
  370.9 8.8 %copy-start.4 = (s32[1,32,24]{1,2,0:T(8,128)S(1)}, s32[1,32,24]{1,2,0:T(8,128)}, u32[]{:S(2)}) copy-start(s32[1,32,24]{1,2,0:T(8,128)} %param.19) | copy-start | bytes 9220
  370.9 80.9 %all-to-all-start.1 = ((bf16[32,32,1536]{2,1,0:T(8,128)(2,1)}), bf16[32,32,1536]{2,1,0:T(8,128)(2,1)S(1)}, u32[]{:S(2)}, u32[]{:S(2)}) async-start(bf16[32,32,1536]{2,1,0:T(8,128)(2,1)} %select_select_fusion), calls=%async_computation.1 | async-start | bytes 6291456 | tf_op jit(solution)/shard_map/all_to_all | solution.py:71
Sparse Core Ops, SparseCore 0:
  33.6 147.0 all-gather.2
